TPU v7x, 256 devices: a whole 4x4x8 slice. The times are simulated.
256 devices in a mesh: fsdp: 16 (over z_hi, x), tensor: 4 (over z_lo, core), replica: 4 (over y).
Axes of the slice: x: 4, y: 4, z: 8 (z_hi: 4, z_lo: 2; z = z_hi * 2 + z_lo), core: 2. Of those that a mesh axis runs over, the one named last changes fastest.
Arguments:
- activations: bfloat16 [24576, 8192], P(('fsdp', 'replica'))
- norm_gain: float32 [8192], replicated, may hold values from 0.1 to 1.9
- key_weight: bfloat16 [8192, 1024], P('fsdp', 'tensor'), may hold values from -0.0625 to 0.0625
- value_weight: bfloat16 [8192, 1024], P('fsdp', 'tensor'), may hold values from -0.0625 to 0.0625
- key_cot: bfloat16 [24576, 1024], P(('fsdp', 'replica'), 'tensor'), may hold values from -6 to 6
- value_cot: bfloat16 [24576, 1024], P(('fsdp', 'replica'), 'tensor'), may hold values from -6 to 6
- blocks: int32 [2, 64, 2], P(None, 'tensor'), may hold values from 0 to 127, as said below
Outputs:
- key_out: bfloat16 [24576, 1024], P(('fsdp', 'replica'), 'tensor')
- value_out: bfloat16 [24576, 1024], P(('fsdp', 'replica'), 'tensor')
- normed_grad: bfloat16 [24576, 8192], P(('fsdp', 'replica'), 'tensor')
- block_grads: float32 [2, 64, 4096], P(None, 'tensor')
Inputs may be any that keep to these rules, and one draw needn't show every extreme that they name: Each run of 16 entries of one projection names 16 distinct blocks of one tensor shard, as (row block below 128, column block below the shard's key columns / 64).
All inputs are finite; a program needn't handle non-finite values.
Results may differ from a plain program's by a relative error of at most 0.013.
Values may be sent and summed in bfloat16 or wider, within the bound.
A program may use at most 128 MiB of HBM per device.

v0:
```python
import jax
import jax.numpy as jnp
from jax import lax
from jax.sharding import PartitionSpec as P

D = 8192
BLK = 64
norm_epsilon = 1e-05


def local(activations, norm_gain, key_weight, value_weight, key_cot, value_cot, blocks):
    tok_rows = activations.shape[0]
    shard_width = key_weight.shape[1]
    widened = activations.astype(jnp.float32)
    inverse_rms = lax.rsqrt(jnp.mean(widened * widened, axis=1, keepdims=True) + norm_epsilon)
    normed = (widened * inverse_rms * norm_gain).astype(jnp.bfloat16)
    stacked = jnp.concatenate([key_weight, value_weight], axis=1)
    cot_both = jnp.concatenate([key_cot, value_cot], axis=1)
    contract_cols = (((1,), (1,)), ((), ()))
    shard_rows = lax.all_gather(stacked, "fsdp", axis=0, tiled=True)
    running = jnp.dot(normed, shard_rows, preferred_element_type=jnp.float32)
    whole = shard_rows
    running, whole = (running, whole)
    partial_value = lax.dot_general(
        cot_both, whole, contract_cols, preferred_element_type=jnp.float32
    ).astype(jnp.bfloat16)
    key_out = running[:, :shard_width].astype(jnp.bfloat16)
    value_out = running[:, shard_width:].astype(jnp.bfloat16)
    normed_grad = (
        lax.psum_scatter(partial_value, "tensor", scatter_dimension=1, tiled=True)
        .astype(jnp.float32)
        .astype(jnp.bfloat16)
    )
    row_index = blocks[:, :, 0].reshape(-1)
    column_index = blocks[:, :, 1]
    left_blocks = jnp.take(normed.reshape(tok_rows, D // BLK, BLK), row_index, axis=1)
    key_blocks = jnp.take(
        key_cot.reshape(tok_rows, shard_width // BLK, BLK), column_index[0], axis=1
    )
    value_blocks = jnp.take(
        value_cot.reshape(tok_rows, shard_width // BLK, BLK), column_index[1], axis=1
    )
    right_blocks = jnp.concatenate([key_blocks, value_blocks], axis=1)
    local_grads = jnp.einsum(
        "tbi,tbj->bij", left_blocks, right_blocks, preferred_element_type=jnp.float32
    )
    local_grads = local_grads.reshape(2, blocks.shape[1], BLK * BLK)
    block_grads = lax.psum(local_grads, ("fsdp", "replica"))
    return (key_out, value_out, normed_grad, block_grads)


def solution(mesh):
    in_specs = (
        P(("fsdp", "replica"), None),
        P(),
        P("fsdp", "tensor"),
        P("fsdp", "tensor"),
        P(("fsdp", "replica"), "tensor"),
        P(("fsdp", "replica"), "tensor"),
        P(None, "tensor", None),
    )
    out_specs = (
        P(("fsdp", "replica"), "tensor"),
        P(("fsdp", "replica"), "tensor"),
        P(("fsdp", "replica"), "tensor"),
        P(None, "tensor", None),
    )
    return jax.shard_map(local, mesh=mesh, in_specs=in_specs, out_specs=out_specs, check_vma=False)
```

profile of v0, /device:TPU:8, one launch (start us, length us, event | category | flops | bytes accessed | tf_op | source)
XLA Modules:
  0.0 862.2 jit_solution(1816326400129489290)
XLA Ops:
  8.0 0.0 all-gather.2.cloned.1.call-start
  8.0 1.9 pad_maximum_fusion
  9.9 0.0 all-gather.2.cloned.1.call-update
  9.9 0.0 all-reduce.2.cloned.1.call-start
  10.0 1.1 copy.12
  11.1 1.1 copy.13
  12.2 0.0 copy-start.2
  12.2 8.7 %copy.11 = bf16[384,8192]{0,1:T(8,128)(2,1)} copy(bf16[384,8192]{1,0:T(8,128)(2,1)} %param.9) | data formatting | bytes 12582912 | tf_op args[0]
  20.9 0.0 copy-done.2
  20.9 0.1 reshape_squeeze.6
  21.0 0.1 reshape_squeeze.5
  21.1 0.0 copy-start.1
  21.1 0.7 gather_fusion.1
  21.8 0.7 gather_fusion.2
  22.6 4.2 fusion
  26.8 0.0 copy-done.1
  26.8 8.2 fusion.2
  35.0 3.8 gather_fusion
  38.7 0.0 copy-start
  38.8 0.2 select_bitcast_fusion
  39.0 0.8 fusion.3
  39.8 1.2 reshape.75
  41.0 0.0 all-reduce.2.cloned.1.call-update
  41.0 0.0 reduce-scatter.2.cloned.1.call-start
  41.0 77.6 %all-gather.2.cloned.1.call-done = bf16[8192,512]{1,0:T(8,128)(2,1)} async-done(((bf16[512,512]{1,0:T(8,128)(2,1)}), bf16[8192,512]{1,0:T(8,128)(2,1)}) %all-gather.2.cloned.1.call-update) | async-done | bytes 8388624 | tf_op jit(solution)/shard_map/all_gather | solution.py:20
  118.6 0.0 copy-done
  118.6 9.7 %convolution_convert_fusion = bf16[384,8192]{1,0:T(8,128)(2,1)} fusion(bf16[8192,512]{1,0:T(8,128)(2,1)} %all-gather.2.cloned.1.call-done, bf16[384,256]{1,0:T(8,128)(2,1)S(1)} %copy-done, bf16[384,256]{1,0:T(8,128)(2,1)} %param.13), kind=kOutput, calls=%fused_computation.8 | convolution fusion | flops 3225157632 | bytes 15073280 | tf_op jit(solution)/shard_map/dot_general | solution.py:24
  128.3 0.0 reduce-scatter.2.cloned.1.call-update
  128.3 8.6 %convolution_convert_fusion.1 = bf16[384,512]{1,0:T(8,128)(2,1)S(1)} fusion(bf16[384,8192]{0,1:T(8,128)(2,1)} %fusion.2, bf16[8192,512]{1,0:T(8,128)(2,1)} %all-gather.2.cloned.1.call-done), kind=kOutput, calls=%fused_computation.16 | convolution fusion | flops 3221422080 | bytes 15073280 | tf_op jit(solution)/shard_map/dot_general | solution.py:21
  136.9 0.8 fusion.18
  137.7 715.1 %all-reduce.2.cloned.1.call-done = f32[2,16,4096]{2,1,0:T(8,128)} async-done(((f32[2,16,4096]{2,1,0:T(8,128)}), f32[2,16,4096]{2,1,0:T(8,128)}) %all-reduce.2.cloned.1.call-update) | async-done | bytes 524304 | tf_op jit(solution)/shard_map/psum | solution.py:48
  852.9 0.0 reduce-scatter.2.cloned.1.call-done
  852.9 1.9 copy.15
  (8 shorter events, 0.1 us)
Async XLA Ops:
  8.0 110.6 %all-gather.2.cloned.1.call-start = ((), (), s32[]{:S(2)}) async-start(), calls=%async_computation.1 | async-start | bytes 8912896 | tf_op jit(solution)/shard_map/all_gather | solution.py:20
  9.9 842.9 %all-reduce.2.cloned.1.call-start = ((), (), s32[]{:S(2)}) async-start(), calls=%async_computation.3 | async-start | bytes 1048576 | tf_op jit(solution)/shard_map/psum | solution.py:48
  12.2 8.7 %copy-start.2 = (s32[2,16,2]{1,2,0:T(2,128)S(1)}, s32[2,16,2]{1,2,0:T(2,128)}, u32[]{:S(2)}) copy-start(s32[2,16,2]{1,2,0:T(2,128)} %param.15) | copy-start | bytes 772
  21.1 5.7 copy-start.1
  38.7 79.9 %copy-start = (bf16[384,256]{1,0:T(8,128)(2,1)S(1)}, bf16[384,256]{1,0:T(8,128)(2,1)}, u32[]{:S(2)}) copy-start(bf16[384,256]{1,0:T(8,128)(2,1)} %param.14) | copy-start | bytes 589828
  41.0 811.9 %reduce-scatter.2.cloned.1.call-start = ((), (), s32[]{:S(2)}) async-start(), calls=%async_computation.2 | async-start | bytes 7864320 | tf_op jit(solution)/shard_map/reduce_scatter | solution.py:30
Sparse Core Ops, SparseCore 0:
  11.8 106.7 all-gather.1
  128.4 76.1 reduce-scatter.1
Sparse Core Ops, SparseCore 1:
  41.1 811.7 all-reduce.1
where the time goes:
time: 863 us; the launch traced here: 862 us
  waiting for transfers between devices  793 us (92%)
  local copies, waits for them, and re-layouts  20.1 us (2%)
  matrix products  19.1 us (2%)
  between operations  15.6 us (2%)
  other arithmetic  14.5 us (2%)
    psum x1, waiting for transfers between devices, local(): block_grads = lax.psum(local_grads, ('fsdp', 'replica'))  715 us
    all_gather x1, waiting for transfers between devices, local(): shard_rows = lax.all_gather(stacked, 'fsdp', axis=0, tiled=True)  77.6 us
  transfers between devices with their start and end apart: 3, of which 2 were waited for; matrix products, arithmetic and copies ran while one was open for 6% of the time, Pallas kernels for 0%

commit v1 on v0

--- a/solution.py
+++ b/solution.py
@@ -45,7 +45,9 @@
         "tbi,tbj->bij", left_blocks, right_blocks, preferred_element_type=jnp.float32
     )
     local_grads = local_grads.reshape(2, blocks.shape[1], BLK * BLK)
-    block_grads = lax.psum(local_grads, ("fsdp", "replica"))
+    block_grads = local_grads
+    for name in ("fsdp", "replica"):
+        block_grads = lax.psum(block_grads, name)
     return (key_out, value_out, normed_grad, block_grads)
 
 

time: 863 us -> 455 us (0.53)
  waiting for transfers between devices: 793 us -> 383 us
    psum x1 -> x2, waiting for transfers between devices: 715 us -> 208 us  [local(): block_grads = lax.psum(block_grads, name)]
    reduce_scatter x1, waiting for transfers between devices: 0.01 us -> 69.9 us  [local(): lax.psum_scatter(partial_value, 'tensor', scatter_dimension=1, tiled=True)]
    all_gather x1, waiting for transfers between devices: 77.6 us -> 105 us  [local(): shard_rows = lax.all_gather(stacked, 'fsdp', axis=0, tiled=True)]
  transfers between devices with their start and end apart: 3 -> 4, of which waited for: 2 -> 4; matrix products, arithmetic and copies ran while one was open for 6% -> 5% of each run, Pallas kernels for 0% -> 0%
where the time goes in v1:
time: 455 us; the launch traced here: 453 us
  waiting for transfers between devices  383 us (84%)
  local copies, waits for them, and re-layouts  20.6 us (5%)
  matrix products  20.2 us (4%)
  other arithmetic  15.1 us (3%)
  between operations  13.9 us (3%)
    psum x2, waiting for transfers between devices, local(): block_grads = lax.psum(block_grads, name)  208 us
    all_gather x1, waiting for transfers between devices, local(): shard_rows = lax.all_gather(stacked, 'fsdp', axis=0, tiled=True)  105 us
    reduce_scatter x1, waiting for transfers between devices, local(): lax.psum_scatter(partial_value, 'tensor', scatter_dimension=1, tiled=True)  69.9 us
    unnamed x10, local copies, waits for them, and re-layouts  12.8 us
    dot_general x1, matrix products, local(): lax.dot_general(cot_both, whole, contract_cols, preferred_element_type=jn...  10.9 us
  transfers between devices with their start and end apart: 4, of which 4 were waited for; matrix products, arithmetic and copies ran while one was open for 5% of the time, Pallas kernels for 0%

profile of v1, /device:TPU:8, one launch (start us, length us, event | category | flops | bytes accessed | tf_op | source)
XLA Modules:
  0.0 453.1 jit_solution(15159295318665513667)
XLA Ops:
  7.2 0.0 all-reduce.3.cloned.1.call-start
  7.2 0.7 compare_and_fusion.1
  7.9 0.7 slice_reduce_fusion
  8.6 1.1 copy.12
  9.7 1.1 copy.13
  10.8 8.7 %copy.11 = bf16[384,8192]{0,1:T(8,128)(2,1)} copy(bf16[384,8192]{1,0:T(8,128)(2,1)} %param.9) | data formatting | bytes 12582912 | tf_op args[0]
  19.5 0.0 copy-start.2
  19.5 4.2 fusion
  23.7 0.1 reshape_squeeze.6
  23.8 0.1 reshape_squeeze.5
  23.9 0.7 gather_fusion.1
  24.6 0.7 gather_fusion.2
  25.4 0.0 copy-done.2
  25.4 8.0 %fusion.2 = bf16[384,8192]{0,1:T(8,128)(2,1)} fusion(bf16[384,8192]{0,1:T(8,128)(2,1)} %copy.11, f32[8192]{0:T(1024)S(1)} %copy-done.2, f32[384]{0:T(512)S(1)} %add_rsqrt_fusion), kind=kLoop, calls=%fused_computation.7 | loop fusion | flops 12582912 | bytes 12617216 | tf_op jit(solution)/shard_map/convert_element_type | solution.py:16
  33.4 3.7 gather_fusion
  37.1 0.2 select_bitcast_fusion
  37.4 0.0 copy-start
  37.4 0.0 copy-start.1
  37.4 0.8 fusion.3
  38.1 1.2 reshape.75
  39.3 0.0 all-reduce.3.cloned.1.call-update
  39.3 0.0 all-gather.2.cloned.1.call-start
  39.4 1.9 pad_maximum_fusion
  41.2 0.0 all-gather.2.cloned.1.call-update
  41.3 0.0 all-reduce.5.cloned.1.call-start
  41.3 167.0 %all-reduce.3.cloned.1.call-done = f32[2,16,4096]{2,1,0:T(8,128)} async-done(((f32[2,16,4096]{2,1,0:T(8,128)}), f32[2,16,4096]{2,1,0:T(8,128)}) %all-reduce.3.cloned.1.call-update) | async-done | bytes 524304 | tf_op jit(solution)/shard_map/psum | solution.py:50
  208.3 0.0 all-reduce.5.cloned.1.call-update
  208.3 0.0 reduce-scatter.2.cloned.1.call-start
  208.4 105.0 %all-gather.2.cloned.1.call-done = bf16[8192,512]{1,0:T(8,128)(2,1)} async-done(((bf16[512,512]{1,0:T(8,128)(2,1)}), bf16[8192,512]{1,0:T(8,128)(2,1)}) %all-gather.2.cloned.1.call-update) | async-done | bytes 8388624 | tf_op jit(solution)/shard_map/all_gather | solution.py:20
  313.4 0.0 copy-done
  313.4 0.0 copy-done.1
  313.4 10.9 %convolution_convert_fusion = bf16[384,8192]{1,0:T(8,128)(2,1)} fusion(bf16[8192,512]{1,0:T(8,128)(2,1)} %all-gather.2.cloned.1.call-done, bf16[384,256]{1,0:T(8,128)(2,1)S(1)} %copy-done, bf16[384,256]{1,0:T(8,128)(2,1)S(1)} %copy-done.1), kind=kOutput, calls=%fused_computation.8 | convolution fusion | flops 3225157632 | bytes 15073280 | tf_op jit(solution)/shard_map/dot_general | solution.py:24
  324.2 0.0 reduce-scatter.2.cloned.1.call-update
  324.2 8.6 %convolution_convert_fusion.1 = bf16[384,512]{1,0:T(8,128)(2,1)S(1)} fusion(bf16[384,8192]{0,1:T(8,128)(2,1)} %fusion.2, bf16[8192,512]{1,0:T(8,128)(2,1)} %all-gather.2.cloned.1.call-done), kind=kOutput, calls=%fused_computation.16 | convolution fusion | flops 3221422080 | bytes 15073280 | tf_op jit(solution)/shard_map/dot_general | solution.py:21
  332.9 0.8 fusion.18
  333.6 41.2 %all-reduce.5.cloned.1.call-done = f32[2,16,4096]{2,1,0:T(8,128)} async-done(((f32[2,16,4096]{2,1,0:T(8,128)}), f32[2,16,4096]{2,1,0:T(8,128)}) %all-reduce.5.cloned.1.call-update) | async-done | bytes 524304 | tf_op jit(solution)/shard_map/psum | solution.py:50
  374.8 69.9 %reduce-scatter.2.cloned.1.call-done = bf16[384,2048]{1,0:T(8,128)(2,1)} async-done(((bf16[384,8192]{1,0:T(8,128)(2,1)}), bf16[384,2048]{1,0:T(8,128)(2,1)}) %reduce-scatter.2.cloned.1.call-update) | async-done | bytes 1572880 | tf_op jit(solution)/shard_map/reduce_scatter | solution.py:30
  444.7 1.9 copy.16
  (6 shorter events, 0.0 us)
Async XLA Ops:
  7.2 201.2 %all-reduce.3.cloned.1.call-start = ((), (), s32[]{:S(2)}) async-start(), calls=%async_computation.3 | async-start | bytes 1048576 | tf_op jit(solution)/shard_map/psum | solution.py:50
  19.5 5.9 %copy-start.2 = (f32[8192]{0:T(1024)S(1)}, f32[8192]{0:T(1024)}, u32[]{:S(2)}) copy-start(f32[8192]{0:T(1024)} %param.10) | copy-start | bytes 98308
  37.4 276.0 %copy-start = (bf16[384,256]{1,0:T(8,128)(2,1)S(1)}, bf16[384,256]{1,0:T(8,128)(2,1)}, u32[]{:S(2)}) copy-start(bf16[384,256]{1,0:T(8,128)(2,1)} %param.14) | copy-start | bytes 589828
  37.4 276.0 %copy-start.1 = (bf16[384,256]{1,0:T(8,128)(2,1)S(1)}, bf16[384,256]{1,0:T(8,128)(2,1)}, u32[]{:S(2)}) copy-start(bf16[384,256]{1,0:T(8,128)(2,1)} %param.13) | copy-start | bytes 589828
  39.3 274.0 %all-gather.2.cloned.1.call-start = ((), (), s32[]{:S(2)}) async-start(), calls=%async_computation.1 | async-start | bytes 8912896 | tf_op jit(solution)/shard_map/all_gather | solution.py:20
  41.3 333.6 %all-reduce.5.cloned.1.call-start = ((), (), s32[]{:S(2)}) async-start(), calls=%async_computation.4 | async-start | bytes 1048576 | tf_op jit(solution)/shard_map/psum | solution.py:50
  208.3 236.4 %reduce-scatter.2.cloned.1.call-start = ((), (), s32[]{:S(2)}) async-start(), calls=%async_computation.2 | async-start | bytes 7864320 | tf_op jit(solution)/shard_map/reduce_scatter | solution.py:30
Sparse Core Ops, SparseCore 0:
  39.4 168.8 all-reduce.2
  211.6 101.6 all-gather.1
  315.8 58.9 all-reduce.4
  378.0 66.6 reduce-scatter.1

commit v2 on v0

--- a/solution.py
+++ b/solution.py
@@ -6,6 +6,11 @@
 D = 8192
 BLK = 64
 norm_epsilon = 1e-05
+
+
+def summed_here(shard, mesh_axis):
+    parts = lax.all_gather(shard, mesh_axis)
+    return jnp.sum(parts, axis=0)
 
 
 def local(activations, norm_gain, key_weight, value_weight, key_cot, value_cot, blocks):
@@ -45,7 +50,7 @@
         "tbi,tbj->bij", left_blocks, right_blocks, preferred_element_type=jnp.float32
     )
     local_grads = local_grads.reshape(2, blocks.shape[1], BLK * BLK)
-    block_grads = lax.psum(local_grads, ("fsdp", "replica"))
+    block_grads = summed_here(local_grads, ("fsdp", "replica"))
     return (key_out, value_out, normed_grad, block_grads)
 
 

time: 863 us -> 494 us (0.57)
  waiting for transfers between devices: 793 us -> 414 us
  other arithmetic: 14.5 us -> 27 us
    psum x1 -> x0, waiting for transfers between devices: 715 us -> none  [local(): block_grads = lax.psum(local_grads, ('fsdp', 'replica'))]
    all_gather x0 -> x1, waiting for transfers between devices: none -> 282 us  [summed_here(): parts = lax.all_gather(shard, mesh_axis)]
    reduce_scatter x1, waiting for transfers between devices: 0.01 us -> 55.4 us  [local(): lax.psum_scatter(partial_value, 'tensor', scatter_dimension=1, tiled=True)]
    reduce_sum x0 -> x1, other arithmetic: none -> 12.5 us  [summed_here(): return jnp.sum(parts, axis=0)]
  transfers between devices with their start and end apart: 3 -> 3, of which waited for: 2 -> 3; matrix products, arithmetic and copies ran while one was open for 6% -> 13% of each run, Pallas kernels for 0% -> 0%
where the time goes in v2:
time: 494 us; the launch traced here: 493 us
  waiting for transfers between devices  414 us (84%)
  other arithmetic  27 us (5%)
  matrix products  19.2 us (4%)
  local copies, waits for them, and re-layouts  18.9 us (4%)
  between operations  13.9 us (3%)
    all_gather x1, waiting for transfers between devices, summed_here(): parts = lax.all_gather(shard, mesh_axis)  282 us
    all_gather x1, waiting for transfers between devices, local(): shard_rows = lax.all_gather(stacked, 'fsdp', axis=0, tiled=True)  76.1 us
    reduce_scatter x1, waiting for transfers between devices, local(): lax.psum_scatter(partial_value, 'tensor', scatter_dimension=1, tiled=True)  55.4 us
    reduce_sum x1, other arithmetic, summed_here(): return jnp.sum(parts, axis=0)  12.5 us
    unnamed x7, local copies, waits for them, and re-layouts  10.9 us
  transfers between devices with their start and end apart: 3, of which 3 were waited for; matrix products, arithmetic and copies ran while one was open for 13% of the time, Pallas kernels for 0%

profile of v2, /device:TPU:8, one launch (start us, length us, event | category | flops | bytes accessed | tf_op | source)
XLA Modules:
  0.0 492.7 jit_solution(14232964200704546445)
XLA Ops:
  7.2 0.0 all-gather.3.cloned.1.call-start
  7.2 1.9 pad_maximum_fusion
  9.1 0.0 all-gather.3.cloned.1.call-update
  9.1 0.0 all-gather.5.cloned.1.call-start
  9.1 0.7 slice_reduce_fusion
  9.8 0.1 reshape_squeeze.5
  9.9 0.1 reshape_squeeze.6
  10.0 1.1 copy.15
  11.1 1.1 copy.16
  12.2 0.0 copy-start.1
  12.2 8.7 %copy.14 = bf16[384,8192]{0,1:T(8,128)(2,1)} copy(bf16[384,8192]{1,0:T(8,128)(2,1)} %param.9) | data formatting | bytes 12582912 | tf_op args[0]
  20.9 0.0 copy-done.1
  20.9 0.0 copy-start
  20.9 0.7 gather_fusion.2
  21.7 0.7 gather_fusion.1
  22.4 4.2 fusion
  26.6 0.0 copy-done
  26.6 8.2 %fusion.2 = bf16[384,8192]{0,1:T(8,128)(2,1)} fusion(bf16[384,8192]{0,1:T(8,128)(2,1)} %copy.14, f32[8192]{0:T(1024)S(1)} %copy-done, f32[384]{0:T(512)S(1)} %add_rsqrt_fusion), kind=kLoop, calls=%fused_computation.7 | loop fusion | flops 12582912 | bytes 12617216 | tf_op jit(solution)/shard_map/convert_element_type | solution.py:21
  34.8 3.8 gather_fusion
  38.6 0.2 select_bitcast_fusion
  38.9 0.8 fusion.3
  39.7 1.2 all_gather_reshape.3
  40.8 0.0 all-gather.5.cloned.1.call-update
  40.9 0.0 reduce-scatter.2.cloned.1.call-start
  40.9 76.1 %all-gather.3.cloned.1.call-done = bf16[8192,512]{1,0:T(8,128)(2,1)} async-done(((bf16[512,512]{1,0:T(8,128)(2,1)}), bf16[8192,512]{1,0:T(8,128)(2,1)}) %all-gather.3.cloned.1.call-update) | async-done | bytes 8388624 | tf_op jit(solution)/shard_map/all_gather | solution.py:25
  117.0 9.8 %convolution_convert_fusion = bf16[384,8192]{1,0:T(8,128)(2,1)} fusion(bf16[8192,512]{1,0:T(8,128)(2,1)} %all-gather.3.cloned.1.call-done, bf16[384,256]{1,0:T(8,128)(2,1)} %param.14, bf16[384,256]{1,0:T(8,128)(2,1)} %param.13), kind=kOutput, calls=%fused_computation.8 | convolution fusion | flops 3225157632 | bytes 15073280 | tf_op jit(solution)/shard_map/dot_general | solution.py:29
  126.8 0.0 reduce-scatter.2.cloned.1.call-update
  126.8 8.6 %convolution_convert_fusion.1 = bf16[384,512]{1,0:T(8,128)(2,1)S(1)} fusion(bf16[384,8192]{0,1:T(8,128)(2,1)} %fusion.2, bf16[8192,512]{1,0:T(8,128)(2,1)} %all-gather.3.cloned.1.call-done), kind=kOutput, calls=%fused_computation.16 | convolution fusion | flops 3221422080 | bytes 15073280 | tf_op jit(solution)/shard_map/dot_general | solution.py:26
  135.4 0.8 fusion.18
  136.2 282.1 %all-gather.5.cloned.1.call-done = f32[64,2,16,4096]{3,2,1,0:T(8,128)} async-done(((f32[1,2,16,4096]{3,2,1,0:T(8,128)}), f32[64,2,16,4096]{3,2,1,0:T(8,128)}) %all-gather.5.cloned.1.call-update) | async-done | bytes 33554448 | tf_op jit(solution)/shard_map/all_gather | solution.py:12
  418.3 12.5 %reduce_sum.19 = f32[2,16,4096]{2,1,0:T(8,128)} reduce(f32[64,2,16,4096]{3,2,1,0:T(8,128)} %all-gather.5.cloned.1.call-done, f32[]{:T(128)} %constant.17.clone.1), dimensions={0}, to_apply=%region_2.0 | reduce | flops 8257536 | bytes 34078724 | tf_op jit(solution)/shard_map/reduce_sum | solution.py:13
  430.8 55.4 %reduce-scatter.2.cloned.1.call-done = bf16[384,2048]{1,0:T(8,128)(2,1)} async-done(((bf16[384,8192]{1,0:T(8,128)(2,1)}), bf16[384,2048]{1,0:T(8,128)(2,1)}) %reduce-scatter.2.cloned.1.call-update) | async-done | bytes 1572880 | tf_op jit(solution)/shard_map/reduce_scatter | solution.py:35
  (7 shorter events, 0.0 us)
Async XLA Ops:
  7.2 109.8 %all-gather.3.cloned.1.call-start = ((), (), s32[]{:S(2)}) async-start(), calls=%async_computation.1 | async-start | bytes 8912896 | tf_op jit(solution)/shard_map/all_gather | solution.py:25
  9.1 409.2 %all-gather.5.cloned.1.call-start = ((), (), s32[]{:S(2)}) async-start(), calls=%async_computation.3 | async-start | bytes 34078720 | tf_op jit(solution)/shard_map/all_gather | solution.py:12
  12.2 8.7 %copy-start.1 = (s32[2,16,2]{1,2,0:T(2,128)S(1)}, s32[2,16,2]{1,2,0:T(2,128)}, u32[]{:S(2)}) copy-start(s32[2,16,2]{1,2,0:T(2,128)} %param.15) | copy-start | bytes 772
  20.9 5.7 %copy-start = (f32[8192]{0:T(1024)S(1)}, f32[8192]{0:T(1024)}, u32[]{:S(2)}) copy-start(f32[8192]{0:T(1024)} %param.10) | copy-start | bytes 98308
  40.9 445.3 %reduce-scatter.2.cloned.1.call-start = ((), (), s32[]{:S(2)}) async-start(), calls=%async_computation.2 | async-start | bytes 7864320 | tf_op jit(solution)/shard_map/reduce_scatter | solution.py:35
Sparse Core Ops, SparseCore 0:
  11.0 105.9 all-gather.2
  120.3 297.9 all-gather.4
  421.5 64.6 reduce-scatter.1
